TPU v7x, 256 devices: a whole 4x4x8 slice. The times are simulated.
256 devices in a mesh: region: 128 (over z_hi, x, y, core), split: 2 (over z_lo).
Axes of the slice: x: 4, y: 4, z: 8 (z_hi: 4, z_lo: 2; z = z_hi * 2 + z_lo), core: 2. Of those that a mesh axis runs over, the one named last changes fastest.
Arguments:
- features: bfloat16 [96, 131072], P(None, ('region', 'split')), may hold values from -6 to 6
- kernel_one: bfloat16 [27, 96, 96], replicated, may hold values from -0.125 to 0.125
- kernel_two: bfloat16 [27, 96, 192], replicated, may hold values from -0.125 to 0.125
- occupancy: int32 [256, 512], P(('region', 'split')), may hold values 0 or 1
- neighbors: int32 [256, 27], P(('region', 'split')), may hold values from -1 to 255, as said below
- cotangent: bfloat16 [192, 131072], P(None, ('region', 'split')), may hold values from -0.016479492 to 0.016479492
Outputs:
- output: bfloat16 [192, 131072], P(None, ('region', 'split'))
- grad_one: float32 [27, 96, 96], replicated
- grad_two: float32 [27, 96, 192], replicated
Inputs may be any that keep to these rules, and one draw needn't show every extreme that they name: `neighbors`: entry k = 9 (dx + 1) + 3 (dy + 1) + (dz + 1) of a block's row is the active block whose block coordinates differ by (dx, dy, dz), or -1 if there is none; entry 13 is the block itself. Blocks are numbered in device order. The blocks of region r have x coordinate r and y coordinate 0 or 1; the device of split index s holds the blocks with z coordinate s. So a neighbour in region r - 1 or r + 1 differs by dx = -1 or +1, and a neighbour on the other device of the same region lies across the z boundary between the two halves.
All inputs are finite; a program needn't handle non-finite values. No bound on the sum of `occupancy` on one device may be relied on, other than what follows from the above.
Results may differ from a plain program's by a relative error of at most 0.0049.
Values may be sent and summed in bfloat16 or wider, within the bound.
A program may use at most 64 MiB of HBM per device.

v0:
```python
import jax
import jax.numpy as jnp
import numpy as np
from jax import lax
from jax.sharding import PartitionSpec as P


def padded(x, sides, width):
    for axis, dim in sides:
        count, length = (lax.axis_size(axis), x.shape[dim])
        up = [(i, (i + 1) % count) for i in range(count - 1)]
        down = [(j, i) for i, j in up]
        last = lax.slice_in_dim(x, length - width, length, axis=dim)
        first = lax.slice_in_dim(x, 0, width, axis=dim)
        before = lax.ppermute(last, axis, up)
        after = lax.ppermute(first, axis, down)
        x = jnp.concatenate([before, x, after], axis=dim)
    return x


def voxel_tables():
    voxels = np.arange(512)
    along_x = voxels // 64
    along_y = voxels // 8 % 8
    along_z = voxels % 8
    block_code = np.zeros((27, 512), np.int32)
    voxel_code = np.zeros((27, 512), np.int32)
    for offset in range(27):
        moved_x = along_x + offset // 9 - 1
        moved_y = along_y + offset // 3 % 3 - 1
        moved_z = along_z + offset % 3 - 1
        block_code[offset] = (moved_x // 8 + 1) * 9 + (moved_y // 8 + 1) * 3 + (moved_z // 8 + 1)
        voxel_code[offset] = moved_x % 8 * 64 + moved_y % 8 * 8 + moved_z % 8
    on_shell = (
        (along_x == 0)
        | (along_x == 7)
        | (along_y == 0)
        | (along_y == 7)
        | (along_z == 0)
        | (along_z == 7)
    )
    shell_voxels = voxels[on_shell].astype(np.int32)
    shell_slot = np.zeros(512, np.int32)
    shell_slot[shell_voxels] = np.arange(shell_voxels.shape[0], dtype=np.int32)
    return (block_code, voxel_code, shell_voxels, shell_slot)


def convolve(window_rows, lookup, kernel):

    def accumulate(offset, total):
        picked = jnp.take(
            window_rows, lax.dynamic_index_in_dim(lookup, offset, 0, keepdims=False), axis=0
        )
        weights = lax.dynamic_index_in_dim(kernel, offset, 0, keepdims=False)
        return total + jnp.dot(picked, weights, preferred_element_type=jnp.float32)

    return lax.fori_loop(
        0, 27, accumulate, jnp.zeros((lookup.shape[1], kernel.shape[2]), jnp.float32)
    )


def kernel_gradient(window_rows, lookup, gradient_rows):

    def accumulate(offset, total):
        picked = jnp.take(
            window_rows, lax.dynamic_index_in_dim(lookup, offset, 0, keepdims=False), axis=0
        )
        product = jnp.dot(picked.T, gradient_rows, preferred_element_type=jnp.float32)
        return lax.dynamic_update_index_in_dim(total, product, offset, 0)

    return lax.fori_loop(
        0,
        27,
        accumulate,
        jnp.zeros((27, window_rows.shape[1], gradient_rows.shape[1]), jnp.float32),
    )


def convolve_back(window_rows, lookup, kernel):

    def accumulate(offset, total):
        picked = jnp.take(
            window_rows, lax.dynamic_index_in_dim(lookup, 26 - offset, 0, keepdims=False), axis=0
        )
        weights = lax.dynamic_index_in_dim(kernel, offset, 0, keepdims=False)
        return total + jnp.dot(picked, weights.T, preferred_element_type=jnp.float32)

    return lax.fori_loop(
        0, 27, accumulate, jnp.zeros((lookup.shape[1], kernel.shape[1]), jnp.float32)
    )


def shards(features, kernel_one, kernel_two, occupancy, neighbors, cotangent):
    block_count = neighbors.shape[0]
    split_size = lax.axis_size("split")
    region_pos = lax.axis_index("region")
    window_first = (region_pos - 1) * split_size * block_count
    block_code, voxel_code, shell_voxels, shell_slot = voxel_tables()
    block_ids = jnp.transpose(jnp.take(neighbors, jnp.asarray(block_code), axis=1), (1, 0, 2))
    voxel_target = jnp.asarray(voxel_code)[:, None, :]
    window_cols = 3 * split_size * block_count * 512
    lookup = jnp.where(block_ids < 0, window_cols, (block_ids - window_first) * 512 + voxel_target)

    def spread(values):
        channels = values.shape[0]
        gathered = lax.all_gather(values, "split", axis=1, tiled=True)
        window = padded(gathered, (("region", 1),), gathered.shape[1])
        return jnp.concatenate([window, jnp.zeros((channels, 1), values.dtype)], axis=1).T

    lookup = lookup.reshape(27, -1).astype(jnp.int32)
    active = (occupancy.reshape(-1) > 0)[None, :]
    zero_value = jnp.zeros((), features.dtype)
    masked = jnp.where(active, features, zero_value)
    masked_window = spread(masked)
    hidden_pre = jnp.where(active, convolve(masked_window, lookup, kernel_one).T, 0.0)
    hidden = jnp.where(active, jax.nn.silu(hidden_pre), 0.0).astype(jnp.bfloat16)
    hidden_window = spread(hidden)
    output = jnp.where(active, convolve(hidden_window, lookup, kernel_two).T, 0.0)
    grad_out = jnp.where(active, cotangent, zero_value)
    grad_two = kernel_gradient(hidden_window, lookup, grad_out.T)
    back = convolve_back(spread(grad_out), lookup, kernel_two).T
    sigmoid_pre = jax.nn.sigmoid(hidden_pre)
    grad_pre = jnp.where(
        active, back * sigmoid_pre * (1.0 + hidden_pre * (1.0 - sigmoid_pre)), 0.0
    ).astype(jnp.bfloat16)
    grad_one = kernel_gradient(masked_window, lookup, grad_pre.T)
    grad_one, grad_two = lax.psum((grad_one, grad_two), ("region", "split"))
    return (output.astype(jnp.bfloat16), grad_one, grad_two)


def solution(mesh):
    in_specs = (
        P(None, ("region", "split")),
        P(),
        P(),
        P(("region", "split"), None),
        P(("region", "split"), None),
        P(None, ("region", "split")),
    )
    out_specs = (P(None, ("region", "split")), P(), P())
    return jax.shard_map(shards, mesh=mesh, in_specs=in_specs, out_specs=out_specs, check_vma=False)
```

profile of v0, /device:TPU:1, one launch (start us, length us, event | category | flops | bytes accessed | tf_op | source)
XLA Modules:
  0.0 732.5 jit_solution(8820615939577342043)
XLA Ops:
  8.8 5.1 all_gather.9
  14.0 5.3 collective-permute-start.1
  22.4 9.6 %all_gather.11 = bf16[192,1024]{0,1:T(8,128)(2,1)S(1)} all-gather(bf16[192,512]{0,1:T(8,128)(2,1)S(1)} %broadcast_select_fusion), channel_id=1, replica_groups=mesh['region'=128,'split'=2] {'split'}, dimensions={1}, use_global_device_ids=true | all-gather | bytes 589824 | tf_op jit(solution)/shard_map/all_gather | solution.py:106
  32.0 3.0 collective-permute-start.5
  35.1 2.5 collective-permute-start.4
  37.6 77.0 %gather_fusion.5 = s32[13824]{0:T(1024)S(1)} fusion(s32[27]{0:T(128)S(1)} %bitcast.83, s32[14336]{0:T(1024)S(1)} %pad_clamp_fusion.5), kind=kCustom, calls=%fused_computation.5 | custom fusion | bytes 165888 | tf_op jit(solution)/shard_map/jit(_take)/gather | solution.py:99
  115.3 67.2 %while.72 = (s32[]{:T(128)}, f32[512,96]{0,1:T(8,128)S(1)}, s32[27,512]{1,0:T(8,128)S(1)}, bf16[3073,96]{1,0:T(8,128)(2,1)S(1)}, bf16[27,96,96]{2,1,0:T(8,128)(2,1)}, /*index=5*/s32[]{:T(128)}, s32[]{:T(128)}) while((s32[]{:T(128)}, f32[512,96]{0,1:T(8,128)S(1)}, s32[27,512]{1,0:T(8,128)S(1)}, bf16[3073,96]{1,0:T(8,128)(2,1)S(1)}, ...), condition=%wide.region_1.3_spmd.clone, body=%wide.region_0.0_spmd.clone.sunk | while | flops 9590275 | bytes 732263 | solution.py:57
  182.6 4.1 all_gather.10
  186.7 3.7 collective-permute-start.3
  198.2 106.1 %while.74 = (s32[]{:T(128)}, f32[512,96]{0,1:T(8,128)}, s32[27,512]{1,0:T(8,128)S(1)}, bf16[3073,192]{1,0:T(8,128)(2,1)S(1)}, bf16[27,96,192]{2,1,0:T(8,128)(2,1...) while((s32[]{:T(128)}, f32[512,96]{0,1:T(8,128)}, s32[27,512]{1,0:T(8,128)S(1)}, ...), condition=%wide.region_5.7_spmd.clone, body=%wide.region_4.6_spmd.clone.sunk | while | flops 19076616 | bytes 1049765 | solution.py:88
  198.2 2.0 gather_fusion.4
  202.0 2.0 gather_fusion.4
  204.0 1.9 convolution_add_fusion.8
  205.9 2.0 gather_fusion.4
  207.9 1.9 convolution_add_fusion.8
  209.9 2.0 gather_fusion.4
  211.8 1.9 convolution_add_fusion.8
  213.8 2.0 gather_fusion.4
  215.8 1.9 convolution_add_fusion.8
  217.7 2.0 gather_fusion.4
  219.7 1.9 convolution_add_fusion.8
  221.7 2.0 gather_fusion.4
  223.6 1.9 convolution_add_fusion.8
  225.6 2.0 gather_fusion.4
  227.6 1.9 convolution_add_fusion.8
  229.5 2.0 gather_fusion.4
  231.5 1.9 convolution_add_fusion.8
  233.5 2.0 gather_fusion.4
  235.4 1.9 convolution_add_fusion.8
  237.4 2.0 gather_fusion.4
  239.4 1.9 convolution_add_fusion.8
  241.4 2.0 gather_fusion.4
  243.3 1.9 convolution_add_fusion.8
  245.3 2.0 gather_fusion.4
  247.2 1.9 convolution_add_fusion.8
  249.2 2.0 gather_fusion.4
  251.2 1.9 convolution_add_fusion.8
  253.2 2.0 gather_fusion.4
  255.1 1.9 convolution_add_fusion.8
  257.1 2.0 gather_fusion.4
  259.1 1.9 convolution_add_fusion.8
  261.0 2.0 gather_fusion.4
  263.0 1.9 convolution_add_fusion.8
  265.0 2.0 gather_fusion.4
  266.9 1.9 convolution_add_fusion.8
  268.9 2.0 gather_fusion.4
  270.9 1.9 convolution_add_fusion.8
  272.8 2.0 gather_fusion.4
  276.8 2.0 gather_fusion.4
  278.7 1.9 convolution_add_fusion.8
  280.7 2.0 gather_fusion.4
  282.7 1.9 convolution_add_fusion.8
  284.6 2.0 gather_fusion.4
  288.6 2.0 gather_fusion.4
  290.5 1.9 convolution_add_fusion.8
  292.5 2.0 gather_fusion.4
  294.5 1.9 convolution_add_fusion.8
  296.4 2.0 gather_fusion.4
  300.4 2.0 gather_fusion.4
  305.5 63.1 %while.70 = (s32[]{:T(128)}, f32[27,96,96]{2,1,0:T(8,128)}, s32[27,512]{1,0:T(8,128)S(1)}, bf16[3073,96]{1,0:T(8,128)(2,1)S(1)}, bf16[512,96]{1,0:T(8,128)(2,1)S(1)}, /*index=5*/s32[]{:T(128)}) while((s32[]{:T(128)}, f32[27,96,96]{2,1,0:T(8,128)}, s32[27,512]{1,0:T(8,128)S(1)}, bf16[3073,96]{1,0:T(8,128)(2,1)S(1)}, ...), condition=%wide.region_7.9_spmd, body=%wide.region_6.8_spmd.sunk | while | flops 9491970 | bytes 461909 | solution.py:71
  368.7 63.7 %while.71 = (s32[]{:T(128)}, f32[27,96,192]{2,1,0:T(8,128)}, s32[27,512]{1,0:T(8,128)S(1)}, bf16[3073,96]{1,0:T(8,128)(2,1)S(1)}, bf16[512,192]{1,0:T(8,128)(2,1)S(1)}, /*index=5*/s32[]{:T(128)}) while((s32[]{:T(128)}, f32[27,96,192]{2,1,0:T(8,128)}, s32[27,512]{1,0:T(8,128)S(1)}, bf16[3073,96]{1,0:T(8,128)(2,1)S(1)}, ...), condition=%wide.region_10.12_spmd, body=%wide.region_9.11_spmd.sunk | while | flops 18929152 | bytes 609365 | solution.py:71
  433.3 69.8 %while.73 = (s32[]{:T(128)}, f32[512,192]{0,1:T(8,128)S(1)}, s32[27,512]{1,0:T(8,128)S(1)}, bf16[3073,96]{1,0:T(8,128)(2,1)S(1)}, bf16[27,96,192]{2,1,0:T(8,128)(2,1)}, /*index=5*/s32[]{:T(128)}, s32[]{:T(128)}) while((s32[]{:T(128)}, f32[512,192]{0,1:T(8,128)S(1)}, s32[27,512]{1,0:T(8,128)S(1)}, bf16[3073,96]{1,0:T(8,128)(2,1)S(1)}, ...), condition=%wide.region_3.5_spmd.clone, body=%wide.region_2.4_spmd.clone.sunk | while | flops 19125764 | bytes 1150055 | solution.py:57
  503.9 217.6 %all-reduce.3.cloned.1.call-done = (f32[27,96,96]{2,1,0:T(8,128)}, f32[27,96,192]{2,1,0:T(8,128)}) async-done(((f32[27,96,96]{2,1,0:T(8,128)}, f32[27,96,192]{2,1,0:T(8,128)}), (f32[27,96,96]{2,1,0:T(8,128)}, f32[27,96,192]{2,1,0:T(8,128)})) %all-reduce.3.cloned.1.call-update) | async-done | bytes 2986000 | tf_op jit(solution)/shard_map/psum | solution.py:127
  721.5 2.6 copy.57
  (786 shorter events, 286.8 us)
Async XLA Ops:
  7.2 30.5 %copy-start = (s32[1,27]{1,0:T(1,128)S(1)}, s32[1,27]{1,0:T(1,128)}, u32[]{:S(2)}) copy-start(s32[1,27]{1,0:T(1,128)} %param.24) | copy-start | bytes 328
  7.2 30.4 %copy-start.7 = (s32[13824]{0:T(1024)S(1)}, s32[13824]{0:T(1024)}, u32[]{:S(2)}) copy-start(s32[13824]{0:T(1024)} %constant.268) | copy-start | bytes 165892
  7.2 714.3 %all-reduce.3.cloned.1.call-start = ((), (), s32[]{:S(2)}) async-start(), calls=%async_computation | async-start | bytes 7962624 | tf_op jit(solution)/shard_map/psum | solution.py:127
  14.0 100.8 %collective-permute-start.1 = (bf16[96,1024]{1,0:T(8,128)(2,1)S(1)}, bf16[96,1024]{1,0:T(8,128)(2,1)S(1)}, u32[]{:S(2)}, u32[]{:S(2)}) collective-permute-start(bf16[96,1024]{1,0:T(8,128)(2,1)S(1)} %all_gather.9), channel_id=1, source_target_pairs={{2,0},{4,2},{6,4},{8,6},{10,8},{12,10},{14,12},{16,14},{18,16},{20... | collective-permute-start | bytes 589832 | tf_op jit(solution)/shard_map/ppermute | solution.py:16
  19.2 95.5 %collective-permute-start = (bf16[96,1024]{1,0:T(8,128)(2,1)S(1)}, bf16[96,1024]{1,0:T(8,128)(2,1)S(1)}, u32[]{:S(2)}, u32[]{:S(2)}) collective-permute-start(bf16[96,1024]{1,0:T(8,128)(2,1)S(1)} %all_gather.9), channel_id=1, source_target_pairs={{0,2},{2,4},{4,6},{6,8},{8,10},{10,12},{12,14},{14,16},{16,18},{18... | collective-permute-start | bytes 589832 | tf_op jit(solution)/shard_map/ppermute | solution.py:15
  32.0 82.6 %copy-start.5 = (bf16[192,1024]{0,1:T(8,128)(2,1)}, bf16[192,1024]{0,1:T(8,128)(2,1)S(1)}, u32[]{:S(2)}) copy-start(bf16[192,1024]{0,1:T(8,128)(2,1)S(1)} %all_gather.11) | copy-start | bytes 1179652
  32.0 163.5 %collective-permute-start.5 = (bf16[192,1024]{0,1:T(8,128)(2,1)S(1)}, bf16[192,1024]{0,1:T(8,128)(2,1)S(1)}, u32[]{:S(2)}, u32[]{:S(2)}) collective-permute-start(bf16[192,1024]{0,1:T(8,128)(2,1)S(1)} %all_gather.11), channel_id=1, source_target_pairs={{2,0},{4,2},{6,4},{8,6},{10,8},{12,10},{14,12},{16,14},{18,16},{20... | collective-permute-start | bytes 1179656 | tf_op jit(solution)/shard_map/ppermute | solution.py:16
  35.1 161.2 %collective-permute-start.4 = (bf16[192,1024]{0,1:T(8,128)(2,1)S(1)}, bf16[192,1024]{0,1:T(8,128)(2,1)}, u32[]{:S(2)}, u32[]{:S(2)}) collective-permute-start(bf16[192,1024]{0,1:T(8,128)(2,1)S(1)} %all_gather.11), channel_id=1, source_target_pairs={{0,2},{2,4},{4,6},{6,8},{8,10},{10,12},{12,14},{14,16},{16,18},{18... | collective-permute-start | bytes 1179656 | tf_op jit(solution)/shard_map/ppermute | solution.py:15
  37.6 77.0 %copy-start.8 = (s32[13824]{0:T(1024)S(1)}, s32[13824]{0:T(1024)}, u32[]{:S(2)}) copy-start(s32[13824]{0:T(1024)} %constant.270) | copy-start | bytes 165892
  182.5 12.5 %copy-start.2 = (f32[512,96]{0,1:T(8,128)}, f32[512,96]{0,1:T(8,128)S(1)}, u32[]{:S(2)}) copy-start(f32[512,96]{0,1:T(8,128)S(1)} %get-tuple-element.512) | copy-start | bytes 589828
  186.7 7.0 collective-permute-start.3
  190.5 4.5 collective-permute-start.2
  195.5 0.8 copy-start.6
  305.5 63.2 %copy-start.3 = (bf16[512,192]{1,0:T(8,128)(2,1)S(1)}, bf16[512,192]{1,0:T(8,128)(2,1)}, u32[]{:S(2)}) copy-start(bf16[512,192]{1,0:T(8,128)(2,1)} %fusion.39) | copy-start | bytes 589828
  432.3 1.0 copy-start.1
  721.5 2.6 copy-start.4
Sparse Core Ops, SparseCore 0:
  432.5 288.9 all-reduce.2
where the time goes:
time: 738 us; the launch traced here: 732 us
  local copies, waits for them, and re-layouts  283 us (38%)
  waiting for transfers between devices  219 us (30%)
  matrix products  164 us (22%)
  blocking collectives  18.9 us (3%)
  starting transfers between devices  18.4 us (2%)
  between operations  14.4 us (2%)
  other arithmetic  9.17 us (1%)
    psum x1, waiting for transfers between devices, shards(): grad_one, grad_two = lax.psum((grad_one, grad_two), ('region', 'split'))  218 us
    gather x108, local copies, waits for them, and re-layouts, accumulate(): jnp.take(window_rows, lax.dynamic_index_in_dim(lookup, offset, 0, keepdim...  145 us
    gather x1, local copies, waits for them, and re-layouts, shards(): jnp.take(neighbors, jnp.asarray(block_code), axis=1)  77 us
    dot_general x54, matrix products, accumulate(): return total + jnp.dot(picked, weights, preferred_element_type=jnp.float32)  59.8 us
    gather x27, local copies, waits for them, and re-layouts, accumulate(): jnp.take(window_rows, lax.dynamic_index_in_dim(lookup, 26 - offset, 0, ke...  52.7 us
    dot_general x27, matrix products, accumulate(): jnp.dot(picked, weights.T, preferred_element_type=jnp.float32)  52.1 us
    dot_general x54, matrix products, accumulate(): jnp.dot(picked.T, gradient_rows, preferred_element_type=jnp.float32)  51.7 us
    all_gather x3, blocking collectives, spread(): gathered = lax.all_gather(values, 'split', axis=1, tiled=True)  18.9 us
  transfers between devices with their start and end apart: 7, of which 3 were waited for; matrix products, arithmetic and copies ran while one was open for 29% of the time, Pallas kernels for 0%

commit v1 on v0

v1 whole, which is shorter than its diff:
```python
import jax
import jax.numpy as jnp
import numpy as np
from jax import lax
from jax.experimental import pallas as pl
from jax.experimental.pallas import tpu as pltpu
from jax.sharding import PartitionSpec as P

MESH = pl.DeviceIdType.MESH
F32 = jnp.float32
BF16 = jnp.bfloat16
C1, C2 = 96, 192
K9 = 9 * C1
SEGS = (1024, 2048)
NCOPY = 5 + 5 + 2 * 34


def one_hots():
    faces = np.zeros((512, 128), np.float32)
    for x in range(8):
        for y in range(8):
            faces[x * 64 + y * 8 + 7, x * 8 + y] = 1
            faces[x * 64 + y * 8, 64 + x * 8 + y] = 1
    rim = [(y, z) for y in range(-1, 9) for z in range(-1, 9) if not (0 <= y < 8 and 0 <= z < 8)]
    rim_lane = {pos: i for i, pos in enumerate(rim)}

    columns = [(xp, y, z) for xp in (-1, 8) for y in range(8) for z in range(8)]
    for planes in (range(-1, 9), range(0, 8)):
        for xp in planes:
            columns += [(xp,) + pos for pos in rim] + [None] * (64 - len(rim))
    place = np.zeros((384, 1280), np.float32)
    offsets = np.zeros((27, 1280), np.float32)
    for n, pos in enumerate(columns):
        if pos is None:
            continue
        xp, y, z = pos
        ex, ey, ez = xp // 8, y // 8, z // 8
        if ex == 0 and ez == 0:
            continue
        offsets[9 * (ex + 1) + 3 * (ey + 1) + ez + 1, n] = 1
        if ex == 0:
            place[256 + (0 if ez < 0 else 64) + xp * 8 + y % 8, n] = 1
        else:
            place[(0 if ez == 0 else 128) + (0 if ex > 0 else 64) + (y % 8) * 8 + z % 8, n] = 1

    shifts = np.zeros((5, 256, 256), np.float32)
    for m in range(9):
        dy, dz = m // 3 - 1, m % 3 - 1
        for half in range(2):
            for y in range(8):
                for z in range(8):
                    col = (m % 2) * 128 + half * 64 + y * 8 + z
                    py, pz = y + dy, z + dz
                    if 0 <= py < 8 and 0 <= pz < 8:
                        row = half * 64 + py * 8 + pz
                    else:
                        row = 128 + half * 64 + rim_lane[(py, pz)]
                    shifts[m // 2, row, col] = 1
    return faces, place, offsets, shifts


def nt_dot(a, b):
    return lax.dot_general(a, b, (((1,), (1,)), ((), ())), preferred_element_type=F32)


def tn_dot(a, b):
    return lax.dot_general(a, b, (((0,), (0,)), ((), ())), preferred_element_type=F32)


def dot(a, b):
    return jnp.dot(a, b, preferred_element_type=F32)


def below(rows, lane):
    return lax.broadcasted_iota(jnp.int32, (rows, 128), 1) < lane


def main_kernel(
    feat_ref, k1_ref, k2_ref, k2b_ref, occ_ref, nb_ref, cot_ref, faces_ref, place_ref, offs_ref, shift_ref,
    out_ref, full1_ref, full2_ref,
    send_a, recv_a, send_h, recv_h, src1, src2, ev1, od1, ev2, od2, evg, odg,
    pk1, pk2, sb1, sb2, rb1, rb2, b11, b12, r11, r12, b21, b22, r21, r22, t21, t22, b31, b32, r31, r32,
    z1, z2, f1, f2, send_sem, recv_sem, out_sem,
):
    reg = lax.axis_index("region")
    s = lax.axis_index("split")
    core = lax.rem(reg, 2)
    y = lax.rem(lax.div(reg, 2), 4)
    x = lax.rem(lax.div(reg, 8), 4)
    zh = lax.div(reg, 32)
    z = zh * 2 + s

    def dev(core_, x_, y_, z_):
        return (((lax.div(z_, 2) * 4 + x_) * 4 + y_) * 2 + core_, lax.rem(z_, 2))

    m1 = x + (y - x) * core
    m2 = y + (x - y) * core
    m1_other = y + (x - y) * core
    partner = dev(1 - core, x, y, z)

    def along1(v):
        return dev(core, x + (v - x) * (1 - core), y + (v - y) * core, z)

    def along2(v):
        return dev(core, x + (v - x) * core, y + (v - y) * (1 - core), z)

    def along_z(v):
        return dev(core, x, y, v)

    up, down = lax.rem(reg + 1, 128), lax.rem(reg + 127, 128)
    halo_peers = ((up, s), (down, s), (up, 1 - s), (down, 1 - s), (reg, 1 - s))

    barrier = pltpu.get_barrier_semaphore()
    peers = list(halo_peers) + [partner]
    peers += [along1(lax.rem(m1 + d, 4)) for d in range(1, 4)]
    peers += [along2(lax.rem(m2 + d, 4)) for d in range(1, 4)]
    peers += [along_z(lax.rem(z + d, 8)) for d in range(1, 8)]
    for peer in peers:
        pl.semaphore_signal(barrier, inc=1, device_id=peer, device_id_type=MESH)

    started = []

    def copy(src, dst, i, peer):
        c = pltpu.make_async_remote_copy(
            src_ref=src, dst_ref=dst, send_sem=send_sem.at[i], recv_sem=recv_sem.at[i],
            device_id=peer, device_id_type=MESH,
        )
        c.start()
        started.append(c)
        return c

    active = (occ_ref[...] > 0).astype(F32)
    masked = (feat_ref[...].astype(F32) * active).astype(BF16)
    grad_out = (cot_ref[...].astype(F32) * active).astype(BF16)

    def send_tiles(own, channels, ref, first):
        tile_x = jnp.where(
            below(channels, 64), own[:, 0:128].astype(F32), own[:, 384:512].astype(F32)
        ).astype(BF16)
        ref[0, first : first + channels, :] = tile_x
        ref[1, first : first + channels, :] = dot(own, faces_ref[...]).astype(BF16)

    send_tiles(masked, C1, send_a, 0)
    send_tiles(grad_out, C2, send_a, C1)
    present = (jnp.broadcast_to(nb_ref[...], (16, 27)) >= 0).astype(F32).astype(BF16)
    flags = dot(present, offs_ref[...])[0:1, :]

    pl.semaphore_wait(barrier, len(peers))

    def send_halo(ref, into, base):
        order = (1, 0, 3, 2, 4)
        return [
            copy(ref.at[0 if q < 4 else 1], into.at[order[q]], base + order[q], halo_peers[q])
            for q in range(5)
        ]

    halo_a = send_halo(send_a, recv_a, 0)

    def gather(own, channels, recv, first, src, even, odd):
        lo = below(channels, 64)
        rows = slice(first, first + channels)

        def joined(p, q):
            return jnp.where(lo, recv[p, rows, :].astype(F32), recv[q, rows, :].astype(F32)).astype(BF16)

        raw = jnp.concatenate([joined(0, 1), joined(2, 3), recv[4, rows, :]], axis=1)
        halo = dot(raw, place_ref[...]) * flags
        ends = halo[:, 0:128]
        halo = halo.astype(BF16)
        rolled = pltpu.roll(own.astype(F32), 64, 1)
        for j in range(9):
            t = j // 2
            if j % 2:
                inner = own[:, t * 128 : (t + 1) * 128]
                rim = halo[:, 768 + t * 128 : 896 + t * 128]
            else:
                if t == 0:
                    inner = jnp.where(lo, ends, rolled[:, 0:128])
                elif t == 4:
                    inner = jnp.where(lo, rolled[:, 0:128], ends)
                else:
                    inner = rolled[:, t * 128 : (t + 1) * 128]
                inner = inner.astype(BF16)
                rim = halo[:, 128 + t * 128 : 256 + t * 128]
            src[j * channels : (j + 1) * channels, 0:128] = inner
            src[j * channels : (j + 1) * channels, 128:256] = rim

        def step(i, carry):
            moved = dot(src[0 : 9 * channels, :], shift_ref[i]).astype(BF16)
            for half in range(2):
                at = pl.ds(pl.multiple_of((2 * i + half) * channels, channels), channels)
                for j in range(9):
                    piece = moved[j * channels : (j + 1) * channels, half * 128 : (half + 1) * 128]
                    t = j // 2
                    if j % 2:
                        even[at, t * 128 : (t + 1) * 128] = piece
                    else:
                        odd[at, t * 128 : (t + 1) * 128] = piece
            return carry

        lax.fori_loop(0, 5, step, 0)

    def group(even, odd, rows, dx):
        if dx == 1:
            return even[rows, :]
        return odd[rows, 0:512] if dx == 0 else odd[rows, 128:640]

    first9 = slice(0, K9)

    def convolve(k_ref, even, odd):
        total = tn_dot(k_ref[0:K9, :], group(even, odd, first9, 0))
        total += tn_dot(k_ref[K9 : 2 * K9, :], group(even, odd, first9, 1))
        total += tn_dot(k_ref[2 * K9 : 3 * K9, :], group(even, odd, first9, 2))
        return total * active

    for c in halo_a:
        c.wait_recv()
    gather(masked, C1, recv_a, 0, src1, ev1, od1)
    hidden_pre = convolve(k1_ref, ev1, od1)
    sig = jax.nn.sigmoid(hidden_pre)
    hidden = (hidden_pre * sig).astype(BF16)
    send_tiles(hidden, C1, send_h, 0)
    halo_h = send_halo(send_h, recv_h, 5)

    gather(grad_out, C2, recv_a, C1, src2, evg, odg)
    back = jnp.zeros((C1, 512), F32)
    for dx in range(3):
        for m in range(9):
            back += dot(k2b_ref[26 - 9 * dx - m], group(evg, odg, slice(m * C2, (m + 1) * C2), dx))
    grad_pre = back * sig * (1.0 + hidden_pre * (1.0 - sig)) * active
    grad_pre = jnp.concatenate([grad_pre, jnp.zeros((32, 512), F32)], axis=0).astype(BF16)
    lo1296 = below(1296, 64)

    grad = jnp.concatenate(
        [nt_dot(group(ev1, od1, first9, dx), grad_pre) for dx in range(3)], axis=0
    )
    pk1[0:1296, :] = jnp.where(lo1296, grad[0:1296], pltpu.roll(grad[1296:2592], 64, 1))
    lane = lax.broadcasted_iota(jnp.int32, (648, 128), 1)
    rest = pltpu.roll(grad[0:648], 64, 1)
    for q in range(1, 4):
        rest = jnp.where(lane < 32 * q, rest, pltpu.roll(grad[648 * q : 648 * (q + 1)], (32 * q + 64) % 128, 1))
    pk1[1296:1944, :] = rest
    pk1[1944:2048, :] = jnp.zeros((104, 128), F32)

    def reduce_steps(h, base, pk, sb, rb, b1, r1, b2, r2, t2, b3, r3, zg, full):
        q1, q2, q3 = h // 4, h // 16, h // 128
        order = (2, 1, 3, 0)
        half = pl.ds(pl.multiple_of((1 - core) * h, h), h)
        sb[...] = pk[half, :].astype(BF16).reshape(4, q1, 128)
        first = []
        for n, d in enumerate(order):
            v = lax.rem(m1_other + d, 4)
            first.append(copy(sb.at[v], rb.at[n], base + n, partner))
        yield
        own = None
        second = []
        for n, d in enumerate(order):
            first[n].wait_recv()
            v = lax.rem(m1 + d, 4)
            part = pk[pl.ds(pl.multiple_of(core * h + v * q1, q1), q1), :] + rb[n].astype(F32)
            if d:
                b1[d - 1] = part.astype(BF16)
                second.append(copy(b1.at[d - 1], r1.at[d - 1], base + 3 + d, along1(v)))
            else:
                own = part
        yield
        for c in second:
            c.wait_recv()
        own = own + r1[0].astype(F32) + r1[1].astype(F32) + r1[2].astype(F32)
        b2[...] = own.reshape(4, q2, 128)
        third = []
        for d in (2, 1, 3):
            v = lax.rem(m2 + d, 4)
            t2[d - 1] = b2[v].astype(BF16)
            third.append(copy(t2.at[d - 1], r2.at[d - 1], base + 6 + d, along2(v)))
        yield
        for c in third:
            c.wait_recv()
        own = b2[m2] + r2[0].astype(F32) + r2[1].astype(F32) + r2[2].astype(F32)
        b3[...] = own.reshape(8, q3, 128)
        fourth = []
        for d in (4, 3, 5, 2, 6, 1, 7):
            v = lax.rem(z + d, 8)
            fourth.append(copy(b3.at[v], r3.at[d - 1], base + 9 + d, along_z(v)))
        yield
        for c in fourth:
            c.wait_recv()
        own = b3[z]
        for d in range(7):
            own = own + r3[d]
        zg[z] = own
        fifth = []
        for d in (4, 3, 5, 2, 6, 1, 7):
            v = lax.rem(z + d, 8)
            fifth.append(copy(zg.at[z], zg.at[z], base + 16 + d, along_z(v)))
        yield
        for c in fifth:
            c.wait_recv()
        full[core, m1, m2] = zg[...].reshape(q2, 128).astype(BF16)
        sixth = []
        for d in (2, 1, 3):
            v = lax.rem(m2 + d, 4)
            sixth.append(copy(full.at[core, m1, m2], full.at[core, m1, m2], base + 23 + d, along2(v)))
        yield
        for c in sixth:
            c.wait_recv()
        seventh = []
        for d in (2, 1, 3):
            v = lax.rem(m1 + d, 4)
            seventh.append(copy(full.at[core, m1], full.at[core, m1], base + 26 + d, along1(v)))
        eighth = [copy(full.at[core, m1], full.at[core, m1], base + 30, partner)]
        yield
        for n, d in ((1, 1), (2, 3), (0, 2)):
            seventh[n].wait_recv()
            v = lax.rem(m1 + 4 - d, 4)
            eighth.append(copy(full.at[core, v], full.at[core, v], base + 30 + d, partner))
        yield
        for c in eighth:
            c.wait_recv()
        yield

    red1 = reduce_steps(SEGS[0], 10, pk1, sb1, rb1, b11, r11, b21, r21, t21, b31, r31, z1, f1)
    next(red1)

    for c in halo_h:
        c.wait_recv()
    gather(hidden, C1, recv_h, 0, src1, ev2, od2)
    next(red1)
    grad = jnp.concatenate(
        [nt_dot(group(ev2, od2, first9, dx), grad_out) for dx in range(3)], axis=0
    )
    pk2[0:2592, :] = grad[:, 0:128]
    tail = jnp.concatenate([grad[:, 128:192], jnp.zeros((2592, 64), F32)], axis=1)
    pk2[2592:3888, :] = jnp.where(lo1296, tail[0:1296], pltpu.roll(tail[1296:2592], 64, 1))
    pk2[3888:4096, :] = jnp.zeros((208, 128), F32)

    red2 = reduce_steps(SEGS[1], 44, pk2, sb2, rb2, b12, r12, b22, r22, t22, b32, r32, z2, f2)
    next(red2)
    next(red1)
    next(red2)
    next(red1)
    out_ref[...] = convolve(k2_ref, ev2, od2).astype(BF16)
    next(red2)
    next(red1)
    next(red2)
    next(red1)
    next(red2)
    next(red1)
    next(red2)
    next(red1)
    next(red2)
    next(red1)
    save1 = pltpu.make_async_copy(f1, full1_ref, out_sem.at[0])
    save1.start()
    next(red2)
    next(red2)
    save2 = pltpu.make_async_copy(f2, full2_ref, out_sem.at[1])
    save2.start()
    for c in started:
        c.wait_send()
    save1.wait()
    save2.wait()


def unpack_kernel(p1_ref, p2_ref, o_ref, g1_ref, g2_ref, out_ref):
    out_ref[...] = o_ref[...]
    g2_ref[:, 0:128] = p2_ref[0:2592, :].astype(F32)
    fold = p2_ref[2592:3888, :].astype(F32)
    g2_ref[0:1296, 128:192] = fold[:, 0:64]
    g2_ref[1296:2592, 128:192] = pltpu.roll(fold, 64, 1)[:, 0:64]
    fold = p1_ref[0:1296, :].astype(F32)
    rest = p1_ref[1296:1944, :].astype(F32)
    both = (fold, pltpu.roll(fold, 64, 1))
    lo = below(648, 64)
    for q in range(4):
        left = both[q // 2][(q % 2) * 648 : (q % 2 + 1) * 648]
        right = pltpu.roll(rest, (64 - 32 * q) % 128, 1)
        g1_ref[648 * q : 648 * (q + 1), :] = jnp.where(lo, left, right)[:, 0:96]


def shards(features, kernel_one, kernel_two, occupancy, neighbors, cotangent):
    faces, place, offsets, shifts = (jnp.asarray(a, BF16) for a in one_hots())
    vmem = pl.BlockSpec(memory_space=pltpu.VMEM)

    def reduce_scratch(h):
        q1, q2, q3 = h // 4, h // 16, h // 128
        return [
            pltpu.VMEM((2 * h, 128), F32),
            pltpu.VMEM((4, q1, 128), BF16),
            pltpu.VMEM((4, q1, 128), BF16),
            pltpu.VMEM((3, q1, 128), BF16),
            pltpu.VMEM((3, q1, 128), BF16),
            pltpu.VMEM((4, q2, 128), F32),
            pltpu.VMEM((3, q2, 128), BF16),
            pltpu.VMEM((3, q2, 128), BF16),
            pltpu.VMEM((8, q3, 128), F32),
            pltpu.VMEM((7, q3, 128), F32),
            pltpu.VMEM((8, q3, 128), F32),
            pltpu.VMEM((2, 4, 4, q2, 128), BF16),
        ]

    pairs = zip(reduce_scratch(SEGS[0]), reduce_scratch(SEGS[1]))
    rows = 10 * C1
    scratch = [
        pltpu.VMEM((2, C1 + C2, 128), BF16),
        pltpu.VMEM((5, C1 + C2, 128), BF16),
        pltpu.VMEM((2, C1, 128), BF16),
        pltpu.VMEM((5, C1, 128), BF16),
        pltpu.VMEM((9 * C1, 256), BF16),
        pltpu.VMEM((9 * C2, 256), BF16),
        pltpu.VMEM((rows, 512), BF16),
        pltpu.VMEM((rows, 640), BF16),
        pltpu.VMEM((rows, 512), BF16),
        pltpu.VMEM((rows, 640), BF16),
        pltpu.VMEM((2 * rows, 512), BF16),
        pltpu.VMEM((2 * rows, 640), BF16),
        *(ref for pair in pairs for ref in pair),
        pltpu.SemaphoreType.DMA((NCOPY,)),
        pltpu.SemaphoreType.DMA((NCOPY,)),
        pltpu.SemaphoreType.DMA((2,)),
    ]
    out, full1, full2 = pl.pallas_call(
        main_kernel,
        out_shape=(
            jax.ShapeDtypeStruct((C2, 512), BF16),
            jax.ShapeDtypeStruct((2, 4, 4, SEGS[0] // 16, 128), BF16),
            jax.ShapeDtypeStruct((2, 4, 4, SEGS[1] // 16, 128), BF16),
        ),
        in_specs=[vmem] * 11,
        out_specs=(vmem, pl.BlockSpec(memory_space=pl.ANY), pl.BlockSpec(memory_space=pl.ANY)),
        scratch_shapes=scratch,
        compiler_params=pltpu.CompilerParams(
            collective_id=0, has_side_effects=True, vmem_limit_bytes=60 * 1024 * 1024
        ),
        name="sparse_conv",
    )(
        features, kernel_one.reshape(27 * C1, C1), kernel_two.reshape(27 * C1, C2), kernel_two,
        occupancy, neighbors, cotangent, faces, place, offsets, shifts,
    )
    grad_one, grad_two, out = pl.pallas_call(
        unpack_kernel,
        out_shape=(
            jax.ShapeDtypeStruct((27 * C1, C1), F32),
            jax.ShapeDtypeStruct((27 * C1, C2), F32),
            jax.ShapeDtypeStruct((C2, 512), BF16),
        ),
        in_specs=[vmem] * 3,
        out_specs=[vmem] * 3,
        name="unpack",
    )(full1.reshape(2 * SEGS[0], 128), full2.reshape(2 * SEGS[1], 128), out)
    return (out, grad_one.reshape(27, C1, C1), grad_two.reshape(27, C1, C2))


def solution(mesh):
    in_specs = (
        P(None, ("region", "split")),
        P(),
        P(),
        P(("region", "split"), None),
        P(("region", "split"), None),
        P(None, ("region", "split")),
    )
    out_specs = (P(None, ("region", "split")), P(), P())
    return jax.shard_map(shards, mesh=mesh, in_specs=in_specs, out_specs=out_specs, check_vma=False)
```

time: 738 us -> 76.3 us (0.10)
  local copies, waits for them, and re-layouts: 283 us -> 0 us
  waiting for transfers between devices: 219 us -> 0 us
  matrix products: 164 us -> 0 us
  Pallas kernels: 0 us -> 75.5 us
  blocking collectives: 18.9 us -> 0 us
  starting transfers between devices: 18.4 us -> 0 us
  between operations: 14.4 us -> 0.64 us
  other arithmetic: 9.17 us -> 0 us
    gather x136 -> x0, local copies, waits for them, and re-layouts: 275 us -> none  [the longest x108 145 us: accumulate(): jnp.take(window_rows, lax.dynamic_index_in_dim(lookup, offset, 0, keepdim...]
    psum x1 -> x0, waiting for transfers between devices: 218 us -> none  [shards(): grad_one, grad_two = lax.psum((grad_one, grad_two), ('region', 'split'))]
    dot_general x135 -> x0, matrix products: 164 us -> none  [the longest x54 59.8 us: accumulate(): return total + jnp.dot(picked, weights, preferred_element_type=jnp.float32)]
    pallas_call x0 -> x2, Pallas kernels: none -> 75.5 us  [the longest x1 71.7 us: shards(): pl.pallas_call(main_kernel, out_shape=(jax.ShapeDtypeStruct((C2, 512), BF...]
    all_gather x3 -> x0, blocking collectives: 18.9 us -> none  [spread(): gathered = lax.all_gather(values, 'split', axis=1, tiled=True)]
    ppermute x6 -> x0, starting transfers between devices: 18.4 us -> none  [the longest x3 12.1 us: padded(): after = lax.ppermute(first, axis, down)]
    unnamed x23 -> x0, local copies, waits for them, and re-layouts: 7.77 us -> none
  transfers between devices with their start and end apart: 7 -> 0, of which waited for: 3 -> 0; matrix products, arithmetic and copies ran while one was open for 29% -> 0% of each run, Pallas kernels for 0% -> 0%
where the time goes in v1:
time: 76.3 us; the launch traced here: 76.2 us
  Pallas kernels  75.5 us (99%)
    pallas_call x1, Pallas kernels, shards(): pl.pallas_call(main_kernel, out_shape=(jax.ShapeDtypeStruct((C2, 512), BF...  71.7 us
    pallas_call x1, Pallas kernels, shards(): pl.pallas_call(unpack_kernel, out_shape=(jax.ShapeDtypeStruct((27 * C1, C...  3.83 us

profile of v1, /device:TPU:1, one launch (start us, length us, event | category | flops | bytes accessed | tf_op | source)
XLA Modules:
  0.0 76.2 jit_solution(52680697115578239)
XLA Ops:
  0.6 71.7 %sparse_conv.1 = (bf16[192,512]{1,0:T(8,128)(2,1)}, bf16[2,4,4,64,128]{4,3,2,1,0:T(8,128)(2,1)}, bf16[2,4,4,128,128]{4,3,2,1,0:T(8,128)(2,1)}) custom-call(bf16[96,512]{1,0:T(8,128)(2,1)} %feat_ref.1, bf16[2592,96]{1,0:T(8,128)(2,1)} %bitcast.8, bf16[2592,192]{1,0:T(8,128)(2,1)} %bitcast.6, bf16[27,96,192]{2,1,0:T(8,128)(2,1)} %k2b_ref.1, s32[1,512]{1,0:T(1,128)} %occ_ref.1, ...), custom_call_target="tpu_custom_call" | custom-call | tf_op jit(solution)/shard_map/sparse_conv/pallas_call | solution.py:422
  72.3 3.8 %unpack.1 = (f32[2592,96]{1,0:T(8,128)}, f32[2592,192]{1,0:T(8,128)}, bf16[192,512]{1,0:T(8,128)(2,1)}) custom-call(bf16[2048,128]{1,0:T(8,128)(2,1)} %bitcast.9, bf16[4096,128]{1,0:T(8,128)(2,1)} %bitcast.7, bf16[192,512]{1,0:T(8,128)(2,1)} %get-tuple-element.11.o_ref), custom_call_target="tpu_custom_call" | custom-call | tf_op jit(solution)/shard_map/unpack/pallas_call | solution.py:440

commit v2 on v1

v2 whole, which is shorter than its diff:
```python
import jax
import jax.numpy as jnp
import numpy as np
from jax import lax
from jax.experimental import pallas as pl
from jax.experimental.pallas import tpu as pltpu
from jax.sharding import PartitionSpec as P

MESH = pl.DeviceIdType.MESH
F32 = jnp.float32
BF16 = jnp.bfloat16
C1, C2 = 96, 192
K9 = 9 * C1
SEGS = (1024, 2048)
VMEM_MIB = 36
NCOPY = 5 + 5 + 2 * 34


def one_hots():
    faces = np.zeros((2, 512, 384), np.float32)
    for split in range(2):
        z = 7 - 7 * split
        for y in range(8):
            for x in range(8):
                for copy in range(2):
                    faces[split, x * 64 + y * 8 + z, copy * 64 + x * 8 + y] = 1
            for copy in range(12):
                faces[split, y * 8 + z, 128 + copy * 8 + y] = 1
                faces[split, 448 + y * 8 + z, 256 + copy * 8 + y] = 1
    rim = [(y, z) for y in range(-1, 9) for z in range(-1, 9) if not (0 <= y < 8 and 0 <= z < 8)]
    rim_lane = {pos: i for i, pos in enumerate(rim)}

    columns = [(xp, y, z) for xp in (-1, 8) for y in range(8) for z in range(8)]
    for planes in (range(-1, 9), range(0, 8)):
        for xp in planes:
            columns += [(xp,) + pos for pos in rim] + [None] * (64 - len(rim))
    place = np.zeros((256, 1280), np.float32)
    offsets = np.zeros((27, 1280), np.float32)
    for n, pos in enumerate(columns):
        if pos is None:
            continue
        xp, y, z = pos
        ex, ey, ez = xp // 8, y // 8, z // 8
        if ex == 0 and ez == 0:
            continue
        offsets[9 * (ex + 1) + 3 * (ey + 1) + ez + 1, n] = 1
        if ex == 0:
            place[128 + xp * 8 + y % 8, n] = 1
        elif ez == 0:
            place[(0 if ex > 0 else 64) + (y % 8) * 8 + z, n] = 1
        else:
            place[192 + (0 if ex > 0 else 8) + y % 8, n] = 1

    shifts = np.zeros((5, 256, 256), np.float32)
    for m in range(9):
        dy, dz = m // 3 - 1, m % 3 - 1
        for half in range(2):
            for y in range(8):
                for z in range(8):
                    col = (m % 2) * 128 + half * 64 + y * 8 + z
                    py, pz = y + dy, z + dz
                    if 0 <= py < 8 and 0 <= pz < 8:
                        row = half * 64 + py * 8 + pz
                    else:
                        row = 128 + half * 64 + rim_lane[(py, pz)]
                    shifts[m // 2, row, col] = 1
    return faces, place, offsets, shifts


def nt_dot(a, b):
    return lax.dot_general(a, b, (((1,), (1,)), ((), ())), preferred_element_type=F32)


def tn_dot(a, b):
    return lax.dot_general(a, b, (((0,), (0,)), ((), ())), preferred_element_type=F32)


def dot(a, b):
    return jnp.dot(a, b, preferred_element_type=F32)


def below(rows, lane):
    return lax.broadcasted_iota(jnp.int32, (rows, 128), 1) < lane


def main_kernel(
    feat_hbm, k1_hbm, k2_hbm, occ_hbm, nb_hbm, cot_hbm, faces_hbm, place_hbm, offs_hbm, shift_hbm,
    out_ref, full1_ref, full2_ref,
    feat_ref, k1_ref, k2_ref, occ_ref, nb_ref, cot_ref, faces_ref, place_ref, offs_ref, shift_ref,
    sx_a, se_a, sz_a, rx_a, re_a, rz_a, sx_h, se_h, sz_h, rx_h, re_h, rz_h,
    src1, src2, ev1, od1, ev2, od2, evg, odg,
    pk1, pk2, sb1, sb2, rb1, rb2, b11, b12, r11, r12, b21, b22, r21, r22, t21, t22,
    b31, b32, t31, t32, r31, r32, f1, f2, send_sem, recv_sem, out_sem, in_sem,
):
    reg = lax.axis_index("region")
    s = lax.axis_index("split")
    core = lax.rem(reg, 2)
    y = lax.rem(lax.div(reg, 2), 4)
    x = lax.rem(lax.div(reg, 8), 4)
    zh = lax.div(reg, 32)
    z = zh * 2 + s

    def dev(core_, x_, y_, z_):
        return (((lax.div(z_, 2) * 4 + x_) * 4 + y_) * 2 + core_, lax.rem(z_, 2))

    m1 = x + (y - x) * core
    m2 = y + (x - y) * core
    m1_other = y + (x - y) * core
    partner = dev(1 - core, x, y, z)

    def along1(v):
        return dev(core, x + (v - x) * (1 - core), y + (v - y) * core, z)

    def along2(v):
        return dev(core, x + (v - x) * core, y + (v - y) * (1 - core), z)

    def along_z(v):
        return dev(core, x, y, v)

    up, down = lax.rem(reg + 1, 128), lax.rem(reg + 127, 128)
    halo_peers = ((up, s), (down, s), (up, 1 - s), (down, 1 - s), (reg, 1 - s))

    barrier = pltpu.get_barrier_semaphore()
    peers = list(halo_peers) + [partner]
    peers += [along1(lax.rem(m1 + d, 4)) for d in range(1, 4)]
    peers += [along2(lax.rem(m2 + d, 4)) for d in range(1, 4)]
    peers += [along_z(lax.rem(z + d, 8)) for d in range(1, 8)]
    for peer in peers:
        pl.semaphore_signal(barrier, inc=1, device_id=peer, device_id_type=MESH)

    loads = {}
    pairs = (
        ("occ", occ_hbm, occ_ref), ("feat", feat_hbm, feat_ref), ("faces", faces_hbm.at[s], faces_ref),
        ("cot", cot_hbm, cot_ref), ("nb", nb_hbm, nb_ref), ("offs", offs_hbm, offs_ref),
        ("place", place_hbm, place_ref), ("shift", shift_hbm, shift_ref),
        ("k1", k1_hbm, k1_ref), ("k2", k2_hbm, k2_ref),
    )
    for i, (name, src, dst) in enumerate(pairs):
        loads[name] = pltpu.make_async_copy(src, dst, in_sem.at[i])
        loads[name].start()

    started = []

    def copy(src, dst, i, peer):
        c = pltpu.make_async_remote_copy(
            src_ref=src, dst_ref=dst, send_sem=send_sem.at[i], recv_sem=recv_sem.at[i],
            device_id=peer, device_id_type=MESH,
        )
        c.start()
        started.append(c)
        return c

    lane8 = lax.broadcasted_iota(jnp.int32, (8, 128), 1)

    def pack_halo(own, rolled, channels, sx, se, sz):
        blocks, half = channels // C1, channels // 2
        lo = below(half, 64)
        mid = 0 if blocks == 1 else C1 // 2
        at = slice(mid, mid + half) if blocks == 2 else slice(0, half)
        picked = dot(own.astype(BF16), faces_ref[...])
        sx[0, at, :] = jnp.where(lo, own[:half, 0:128], rolled[half:, 0:128]).astype(BF16)
        sx[1, at, :] = jnp.where(lo, rolled[:half, 0:128], own[half:, 384:512]).astype(BF16)
        sz[at, :] = jnp.where(lo, picked[:half, 0:128], picked[half:, 0:128]).astype(BF16)
        for b in range(blocks):
            to = (b + blocks - 1) * 8
            for q in range(2):
                edge = jnp.zeros((8, 128), F32)
                for g in range(12):
                    rows = slice(b * C1 + g * 8, b * C1 + g * 8 + 8)
                    edge = jnp.where(lax.div(lane8, 8) == g, picked[rows, 128 + 128 * q : 256 + 128 * q], edge)
                se[q, to : to + 8, :] = edge.astype(BF16)

    def unpack_halo(channels, rx, re, rz):
        blocks, half = channels // C1, channels // 2
        lo = below(half, 64)
        mid = 0 if blocks == 1 else C1 // 2
        at = slice(mid, mid + half)
        above, under, face = rx[0, at, :].astype(F32), rx[1, at, :].astype(F32), rz[at, :].astype(F32)
        planes = jnp.concatenate(
            [jnp.where(lo, above, pltpu.roll(under, 64, 1)), jnp.where(lo, pltpu.roll(above, 64, 1), under)], axis=0
        )
        face = jnp.concatenate([face, pltpu.roll(face, 64, 1)], axis=0)
        edges = []
        for b in range(blocks):
            rows = slice((b + blocks - 1) * 8, (b + blocks) * 8)
            above, under = re[0, rows, :].astype(F32), re[1, rows, :].astype(F32)
            for g in range(12):
                a = pltpu.roll(above, (64 - 8 * g) % 128, 1)
                u = pltpu.roll(under, (72 - 8 * g) % 128, 1)
                edges.append(jnp.where(lane8 < 72, a, u))
        side = jnp.where(below(channels, 64), face, jnp.concatenate(edges, axis=0))
        return jnp.concatenate([planes, side], axis=1).astype(BF16)

    def send_halo(sx, se, sz, rx, re, rz, base):
        return [
            copy(se.at[1], re.at[1], base, halo_peers[2]),
            copy(se.at[0], re.at[0], base + 1, halo_peers[3]),
            copy(sz, rz, base + 2, halo_peers[4]),
            copy(sx.at[1], rx.at[1], base + 3, halo_peers[0]),
            copy(sx.at[0], rx.at[0], base + 4, halo_peers[1]),
        ]

    loads["occ"].wait()
    loads["feat"].wait()
    loads["faces"].wait()
    active = (occ_ref[...] > 0).astype(F32)
    masked = feat_ref[...].astype(F32) * active
    masked_rolled = pltpu.roll(masked, 64, 1)
    pack_halo(masked, masked_rolled, C1, sx_a, se_a, sz_a)
    loads["cot"].wait()
    grad_wide = cot_ref[...].astype(F32) * active
    grad_rolled = pltpu.roll(grad_wide, 64, 1)
    pack_halo(grad_wide, grad_rolled, C2, sx_a, se_a, sz_a)
    grad_out = grad_wide.astype(BF16)
    loads["nb"].wait()
    loads["offs"].wait()
    present = (jnp.broadcast_to(nb_ref[...], (16, 27)) >= 0).astype(F32).astype(BF16)
    flags = dot(present, offs_ref[...])[0:1, :]

    pl.semaphore_wait(barrier, len(peers))
    halo_a = send_halo(sx_a, se_a, sz_a, rx_a, re_a, rz_a, 0)
    for name in ("place", "shift", "k1", "k2"):
        loads[name].wait()

    def gather(own, rolled, raw, channels, src, even, odd):
        lo = below(channels, 64)
        halo = dot(raw, place_ref[...]) * flags
        ends = halo[:, 0:128]
        halo = halo.astype(BF16)
        for j in range(9):
            t = j // 2
            if j % 2:
                inner = own[:, t * 128 : (t + 1) * 128]
                rim = halo[:, 768 + t * 128 : 896 + t * 128]
            else:
                inner = rolled[:, (t % 4) * 128 : (t % 4 + 1) * 128]
                if t == 0:
                    inner = jnp.where(lo, ends, inner)
                elif t == 4:
                    inner = jnp.where(lo, inner, ends)
                rim = halo[:, 128 + t * 128 : 256 + t * 128]
            src[j * channels : (j + 1) * channels, 0:128] = inner.astype(BF16)
            src[j * channels : (j + 1) * channels, 128:256] = rim

        def step(i, carry):
            moved = dot(src[...], shift_ref[i]).astype(BF16)
            for half in range(2):
                at = pl.ds(pl.multiple_of((2 * i + half) * channels, channels), channels)
                for j in range(9):
                    piece = moved[j * channels : (j + 1) * channels, half * 128 : (half + 1) * 128]
                    t = j // 2
                    if j % 2:
                        even[at, t * 128 : (t + 1) * 128] = piece
                    else:
                        odd[at, t * 128 : (t + 1) * 128] = piece
            return carry

        lax.fori_loop(0, 5, step, 0)

    def group(even, odd, rows, dx):
        if dx == 1:
            return even[rows, :]
        return odd[rows, 0:512] if dx == 0 else odd[rows, 128:640]

    first9 = slice(0, K9)

    def convolve(weights, even, odd):
        total = tn_dot(weights(0), group(even, odd, first9, 0))
        total += tn_dot(weights(1), group(even, odd, first9, 1))
        total += tn_dot(weights(2), group(even, odd, first9, 2))
        return total * active

    for c in halo_a:
        c.wait_recv()
    gather(masked, masked_rolled, unpack_halo(C1, rx_a, re_a, rz_a), C1, src1, ev1, od1)
    hidden_pre = convolve(lambda dx: k1_ref[dx * K9 : (dx + 1) * K9, :], ev1, od1)
    sig = jax.nn.sigmoid(hidden_pre)
    hidden = (hidden_pre * sig).astype(BF16).astype(F32)
    hidden_rolled = pltpu.roll(hidden, 64, 1)
    pack_halo(hidden, hidden_rolled, C1, sx_h, se_h, sz_h)
    halo_h = send_halo(sx_h, se_h, sz_h, rx_h, re_h, rz_h, 5)

    gather(grad_wide, grad_rolled, unpack_halo(C2, rx_a, re_a, rz_a), C2, src2, evg, odg)
    lo1296 = below(1296, 64)

    def reduce_steps(h, base, pk, sb, rb, b1, r1, b2, r2, t2, b3, t3, r3, full):
        q1, q2, q3 = h // 4, h // 16, h // 128
        order = (2, 1, 3, 0)
        half = pl.ds(pl.multiple_of((1 - core) * h, h), h)
        sb[...] = pk[half, :].astype(BF16).reshape(4, q1, 128)
        first = []
        for n, d in enumerate(order):
            v = lax.rem(m1_other + d, 4)
            first.append(copy(sb.at[v], rb.at[n], base + n, partner))
        yield
        own = None
        second = []
        for n, d in enumerate(order):
            first[n].wait_recv()
            v = lax.rem(m1 + d, 4)
            part = pk[pl.ds(pl.multiple_of(core * h + v * q1, q1), q1), :] + rb[n].astype(F32)
            if d:
                b1[d - 1] = part.astype(BF16)
                second.append(copy(b1.at[d - 1], r1.at[d - 1], base + 3 + d, along1(v)))
            else:
                own = part
        yield
        for c in second:
            c.wait_recv()
        own = own + r1[0].astype(F32) + r1[1].astype(F32) + r1[2].astype(F32)
        b2[...] = own.reshape(4, q2, 128)
        third = []
        for d in (2, 1, 3):
            v = lax.rem(m2 + d, 4)
            t2[d - 1] = b2[v].astype(BF16)
            third.append(copy(t2.at[d - 1], r2.at[d - 1], base + 6 + d, along2(v)))
        yield
        for c in third:
            c.wait_recv()
        own = b2[m2] + r2[0].astype(F32) + r2[1].astype(F32) + r2[2].astype(F32)
        b3[...] = own.reshape(8, q3, 128)
        t3[...] = own.reshape(8, q3, 128).astype(BF16)
        fourth = []
        for d in (4, 3, 5, 2, 6, 1, 7):
            v = lax.rem(z + d, 8)
            fourth.append(copy(t3.at[v], r3.at[d - 1], base + 9 + d, along_z(v)))
        yield
        for c in fourth:
            c.wait_recv()
        own = b3[z]
        for d in range(7):
            own = own + r3[d].astype(F32)
        full[core, m1, m2, z] = own.astype(BF16)
        mine = full.at[core, m1, m2, z]
        fifth = []
        for d in (4, 3, 5, 2, 6, 1, 7):
            v = lax.rem(z + d, 8)
            fifth.append(copy(mine, mine, base + 16 + d, along_z(v)))
        yield
        for c in fifth:
            c.wait_recv()
        mine = full.at[core, m1, m2]
        sixth = []
        for d in (2, 1, 3):
            v = lax.rem(m2 + d, 4)
            sixth.append(copy(mine, mine, base + 23 + d, along2(v)))
        yield
        for c in sixth:
            c.wait_recv()
        seventh = []
        for d in (2, 1, 3):
            v = lax.rem(m1 + d, 4)
            seventh.append(copy(full.at[core, m1], full.at[core, m1], base + 26 + d, along1(v)))
        eighth = [copy(full.at[core, m1], full.at[core, m1], base + 30, partner)]
        yield
        for n, d in ((1, 1), (2, 3), (0, 2)):
            seventh[n].wait_recv()
            v = lax.rem(m1 + 4 - d, 4)
            eighth.append(copy(full.at[core, v], full.at[core, v], base + 30 + d, partner))
        yield
        for c in eighth:
            c.wait_recv()
        yield

    red1 = reduce_steps(SEGS[0], 10, pk1, sb1, rb1, b11, r11, b21, r21, t21, b31, t31, r31, f1)
    red2 = reduce_steps(SEGS[1], 44, pk2, sb2, rb2, b12, r12, b22, r22, t22, b32, t32, r32, f2)

    for c in halo_h:
        c.wait_recv()
    gather(hidden, hidden_rolled, unpack_halo(C1, rx_h, re_h, rz_h), C1, src1, ev2, od2)
    grad = jnp.concatenate(
        [nt_dot(group(ev2, od2, first9, dx), grad_out) for dx in range(3)], axis=0
    )
    pk2[0:2592, :] = grad[:, 0:128]
    tail = jnp.concatenate([grad[:, 128:192], jnp.zeros((2592, 64), F32)], axis=1)
    pk2[2592:3888, :] = jnp.where(lo1296, tail[0:1296], pltpu.roll(tail[1296:2592], 64, 1))
    pk2[3888:4096, :] = jnp.zeros((208, 128), F32)
    next(red2)

    back = jnp.zeros((C1, 512), F32)
    for dx in range(3):
        for m in range(9):
            back += dot(k2_ref[26 - 9 * dx - m], group(evg, odg, slice(m * C2, (m + 1) * C2), dx))
    grad_pre = back * sig * (1.0 + hidden_pre * (1.0 - sig)) * active
    grad_pre = jnp.concatenate([grad_pre, jnp.zeros((32, 512), F32)], axis=0).astype(BF16)
    next(red2)
    grad = jnp.concatenate(
        [nt_dot(group(ev1, od1, first9, dx), grad_pre) for dx in range(3)], axis=0
    )
    pk1[0:1296, :] = jnp.where(lo1296, grad[0:1296], pltpu.roll(grad[1296:2592], 64, 1))
    lane = lax.broadcasted_iota(jnp.int32, (648, 128), 1)
    rest = pltpu.roll(grad[0:648], 64, 1)
    for q in range(1, 4):
        rest = jnp.where(lane < 32 * q, rest, pltpu.roll(grad[648 * q : 648 * (q + 1)], (32 * q + 64) % 128, 1))
    pk1[1296:1944, :] = rest
    pk1[1944:2048, :] = jnp.zeros((104, 128), F32)
    next(red1)
    next(red1)
    out_ref[...] = convolve(
        lambda dx: k2_ref[9 * dx : 9 * dx + 9].reshape(K9, C2), ev2, od2
    ).astype(BF16)
    next(red2)
    next(red1)
    next(red2)
    next(red1)
    next(red2)
    next(red1)
    next(red2)
    next(red1)
    next(red2)
    next(red1)
    next(red2)
    next(red1)
    next(red2)
    save2 = pltpu.make_async_copy(f2, full2_ref, out_sem.at[1])
    save2.start()
    next(red1)
    save1 = pltpu.make_async_copy(f1, full1_ref, out_sem.at[0])
    save1.start()
    for c in started:
        c.wait_send()
    save2.wait()
    save1.wait()


def unpack_kernel(
    p1_hbm, p2_hbm, o_hbm, g1_hbm, g2_hbm, out_hbm, p1_ref, p2_ref, o_ref, g1_ref, g2_ref, in_sem, out_sem
):
    loads = [
        pltpu.make_async_copy(src, dst, in_sem.at[i])
        for i, (src, dst) in enumerate(((p2_hbm, p2_ref), (p1_hbm, p1_ref), (o_hbm, o_ref)))
    ]
    for c in loads:
        c.start()
    stores = []

    def store(src, dst):
        stores.append(pltpu.make_async_copy(src, dst, out_sem.at[len(stores)]))
        stores[-1].start()

    loads[0].wait()
    for q in range(4):
        rows = slice(648 * q, 648 * (q + 1))
        g2_ref[rows, 0:128] = p2_ref[rows, :].astype(F32)
        fold = p2_ref[2592 + (q % 2) * 648 : 3240 + (q % 2) * 648, :].astype(F32)
        if q > 1:
            fold = pltpu.roll(fold, 64, 1)
        g2_ref[rows, 128:192] = fold[:, 0:64]
        store(g2_ref.at[rows], g2_hbm.at[rows])
    loads[1].wait()
    lo = below(648, 64)
    for q in range(4):
        rows = slice(648 * q, 648 * (q + 1))
        left = p1_ref[(q % 2) * 648 : (q % 2 + 1) * 648, :].astype(F32)
        if q > 1:
            left = pltpu.roll(left, 64, 1)
        right = pltpu.roll(p1_ref[1296:1944, :].astype(F32), (64 - 32 * q) % 128, 1)
        g1_ref[rows, :] = jnp.where(lo, left, right)[:, 0:96]
        store(g1_ref.at[rows], g1_hbm.at[rows])
    loads[2].wait()
    store(o_ref, out_hbm)
    for c in stores:
        c.wait()


def shards(features, kernel_one, kernel_two, occupancy, neighbors, cotangent):
    faces, place, offsets, shifts = (jnp.asarray(a, BF16) for a in one_hots())
    hbm, any_ = pl.BlockSpec(memory_space=pltpu.HBM), pl.BlockSpec(memory_space=pl.ANY)
    vmem = pl.BlockSpec(memory_space=pltpu.VMEM)

    def reduce_scratch(h):
        q1, q2, q3 = h // 4, h // 16, h // 128
        return [
            pltpu.VMEM((2 * h, 128), F32),
            pltpu.VMEM((4, q1, 128), BF16),
            pltpu.VMEM((4, q1, 128), BF16),
            pltpu.VMEM((3, q1, 128), BF16),
            pltpu.VMEM((3, q1, 128), BF16),
            pltpu.VMEM((4, q2, 128), F32),
            pltpu.VMEM((3, q2, 128), BF16),
            pltpu.VMEM((3, q2, 128), BF16),
            pltpu.VMEM((8, q3, 128), F32),
            pltpu.VMEM((8, q3, 128), BF16),
            pltpu.VMEM((7, q3, 128), BF16),
            pltpu.VMEM((2, 4, 4, 8, q3, 128), BF16),
        ]

    pairs = zip(reduce_scratch(SEGS[0]), reduce_scratch(SEGS[1]))
    rows = 10 * C1

    def halo_scratch(channels):
        half, edge = channels // 2, channels // 12
        return 2 * [
            pltpu.VMEM((2, half, 128), BF16),
            pltpu.VMEM((2, edge, 128), BF16),
            pltpu.VMEM((half, 128), BF16),
        ]

    scratch = [
        pltpu.VMEM((C1, 512), BF16),
        pltpu.VMEM((27 * C1, C1), BF16),
        pltpu.VMEM((27, C1, C2), BF16),
        pltpu.VMEM((1, 512), jnp.int32),
        pltpu.VMEM((1, 27), jnp.int32),
        pltpu.VMEM((C2, 512), BF16),
        pltpu.VMEM((512, 384), BF16),
        pltpu.VMEM((256, 1280), BF16),
        pltpu.VMEM((27, 1280), BF16),
        pltpu.VMEM((5, 256, 256), BF16),
        *halo_scratch(C1 + C2),
        *halo_scratch(C1),
        pltpu.VMEM((9 * C1, 256), BF16),
        pltpu.VMEM((9 * C2, 256), BF16),
        pltpu.VMEM((rows, 512), BF16),
        pltpu.VMEM((rows, 640), BF16),
        pltpu.VMEM((rows, 512), BF16),
        pltpu.VMEM((rows, 640), BF16),
        pltpu.VMEM((2 * rows, 512), BF16),
        pltpu.VMEM((2 * rows, 640), BF16),
        *(ref for pair in pairs for ref in pair),
        pltpu.SemaphoreType.DMA((NCOPY,)),
        pltpu.SemaphoreType.DMA((NCOPY,)),
        pltpu.SemaphoreType.DMA((2,)),
        pltpu.SemaphoreType.DMA((10,)),
    ]
    out, full1, full2 = pl.pallas_call(
        main_kernel,
        out_shape=(
            jax.ShapeDtypeStruct((C2, 512), BF16),
            jax.ShapeDtypeStruct((2, 4, 4, 8, SEGS[0] // 128, 128), BF16),
            jax.ShapeDtypeStruct((2, 4, 4, 8, SEGS[1] // 128, 128), BF16),
        ),
        in_specs=[hbm] * 10,
        out_specs=(vmem, any_, any_),
        scratch_shapes=scratch,
        compiler_params=pltpu.CompilerParams(
            collective_id=0, has_side_effects=True, vmem_limit_bytes=VMEM_MIB << 20
        ),
        name="sparse_conv",
    )(
        *(
            pltpu.with_memory_space_constraint(a, pltpu.HBM)
            for a in (
                features, kernel_one.reshape(27 * C1, C1), kernel_two,
                occupancy, neighbors, cotangent, faces, place, offsets, shifts,
            )
        )
    )
    grad_one, grad_two, out = pl.pallas_call(
        unpack_kernel,
        out_shape=(
            jax.ShapeDtypeStruct((27 * C1, C1), F32),
            jax.ShapeDtypeStruct((27 * C1, C2), F32),
            jax.ShapeDtypeStruct((C2, 512), BF16),
        ),
        in_specs=[any_] * 3,
        out_specs=[hbm] * 3,
        scratch_shapes=[
            pltpu.VMEM((2 * SEGS[0], 128), BF16),
            pltpu.VMEM((2 * SEGS[1], 128), BF16),
            pltpu.VMEM((C2, 512), BF16),
            pltpu.VMEM((27 * C1, C1), F32),
            pltpu.VMEM((27 * C1, C2), F32),
            pltpu.SemaphoreType.DMA((3,)),
            pltpu.SemaphoreType.DMA((9,)),
        ],
        compiler_params=pltpu.CompilerParams(vmem_limit_bytes=16 << 20),
        name="unpack",
    )(full1.reshape(2 * SEGS[0], 128), full2.reshape(2 * SEGS[1], 128), out)
    return (out, grad_one.reshape(27, C1, C1), grad_two.reshape(27, C1, C2))


def solution(mesh):
    in_specs = (
        P(None, ("region", "split")),
        P(),
        P(),
        P(("region", "split"), None),
        P(("region", "split"), None),
        P(None, ("region", "split")),
    )
    out_specs = (P(None, ("region", "split")), P(), P())
    return jax.shard_map(shards, mesh=mesh, in_specs=in_specs, out_specs=out_specs, check_vma=False)
```

time: 76.3 us -> 67 us (0.88)
  Pallas kernels: 75.5 us -> 66.3 us
    pallas_call x1, Pallas kernels: 71.7 us -> 63.8 us  [shards(): pl.pallas_call(main_kernel, out_shape=(jax.ShapeDtypeStruct((C2, 512), BF...]
    pallas_call x1, Pallas kernels: 3.83 us -> 2.52 us  [shards(): pl.pallas_call(unpack_kernel, out_shape=(jax.ShapeDtypeStruct((27 * C1, C...]
where the time goes in v2:
time: 67 us; the launch traced here: 66.9 us
  Pallas kernels  66.3 us (99%)
    pallas_call x1, Pallas kernels, shards(): pl.pallas_call(main_kernel, out_shape=(jax.ShapeDtypeStruct((C2, 512), BF...  63.8 us
    pallas_call x1, Pallas kernels, shards(): pl.pallas_call(unpack_kernel, out_shape=(jax.ShapeDtypeStruct((27 * C1, C...  2.52 us

profile of v2, /device:TPU:1, one launch (start us, length us, event | category | flops | bytes accessed | tf_op | source)
XLA Modules:
  0.0 66.9 jit_solution(4610267120044661729)
XLA Ops:
  0.6 63.8 %sparse_conv.1 = (bf16[192,512]{1,0:T(8,128)(2,1)S(1)}, bf16[2,4,4,8,8,128]{5,4,3,2,1,0:T(8,128)(2,1)S(1)}, bf16[2,4,4,8,16,128]{5,4,3,2,1,0:T(8,128)(2,1)S(1)}) custom-call(bf16[96,512]{1,0:T(8,128)(2,1)} %feat_hbm.1, bf16[2592,96]{1,0:T(8,128)(2,1)} %bitcast.7, bf16[27,96,192]{2,1,0:T(8,128)(2,1)} %k2_hbm.1, s32[1,512]{1,0:T(1,128)} %occ_hbm.1, ...), custom_call_target="tpu_custom_call" | custom-call | tf_op jit(solution)/shard_map/sparse_conv/pallas_call | solution.py:526
  64.4 2.5 %unpack.1 = (f32[2592,96]{1,0:T(8,128)}, f32[2592,192]{1,0:T(8,128)}, bf16[192,512]{1,0:T(8,128)(2,1)}) custom-call(bf16[2048,128]{1,0:T(8,128)(2,1)S(1)} %bitcast.6, bf16[4096,128]{1,0:T(8,128)(2,1)S(1)} %bitcast.5, bf16[192,512]{1,0:T(8,128)(2,1)S(1)} %get-tuple-element.11.o_hbm), custom_call_target="tpu_custom_call" | custom-call | tf_op jit(solution)/shard_map/unpack/pallas_call | solution.py:549
